TPU v7x, 32 devices: a whole 2x2x4 slice. The times are simulated.
32 devices in a mesh: wide: 8 (over z, x), narrow: 4 (over y, core).
Axes of the slice: x: 2, y: 2, z: 4, core: 2. Of those that a mesh axis runs over, the one named last changes fastest.
Arguments:
- samples: bfloat16 [16384, 1024], P(('wide', 'narrow')), may hold values from -16 to 16
- centroid_table: bfloat16 [16384, 1024], P('wide', 'narrow'), may hold values from -6 to 6
- owner: int32 [16384], replicated, may hold values from 0 to 7, as said below
- slot: int32 [16384], replicated, may hold values from 0 to 2047, as said below
- assign: int32 [16384], P('wide'), may hold values from 0 to 16383, as said below
- codebook: float32 [8, 2048, 128], P('narrow'), may hold values from -16 to 16
Outputs:
- residual: bfloat16 [16384, 1024], P('wide', 'narrow')
- refined: float32 [8, 2048, 128], P('narrow')
Inputs may be any that keep to these rules, and one draw needn't show every extreme that they name: owner and slot give each coarse centroid a distinct storage position owner * 2048 + slot. `slot`: see owner. `assign`: in each aligned block of 2048 rows (the rows of one index of wide), at most 512 rows have centroids with one owner, and some owner has exactly 512.
All inputs are finite; a program needn't handle non-finite values.
Results may differ from a plain program's by a relative error of at most 0.0079.
Values may be sent and summed in bfloat16 or wider, within the bound.
No kernel may reach another device: no remote copies, remote signals or barrier semaphores. Data moves between devices by JAX's collectives and lax.ppermute only.
A program may use at most 64 MiB of HBM per device.

v0:
```python
import jax
import jax.numpy as jnp
from jax import lax
from jax.sharding import PartitionSpec as P

ITERS = 2


softness_level = 16.0
prior_weight = 1.0


def score_pass(blocks, narrow_words, codeword_norm_values):
    spaces = narrow_words.shape[0]
    words_count = narrow_words.shape[1]
    sub_width = narrow_words.shape[2]

    def block_step(running, row_block):
        inner_product_rows = jnp.einsum(
            "bms,mks->mbk", row_block, narrow_words, preferred_element_type=jnp.float32
        )
        score_matrix = (
            2.0 * inner_product_rows - codeword_norm_values[:, None, :]
        ) / softness_level
        weights_soft = jax.nn.softmax(score_matrix, axis=2).astype(jnp.bfloat16)
        totals = running[0] + jnp.einsum(
            "mbk,bms->mks", weights_soft, row_block, preferred_element_type=jnp.float32
        )
        return ((totals, running[1] + jnp.sum(weights_soft, axis=1, dtype=jnp.float32)), None)

    start = (
        jnp.zeros((spaces, words_count, sub_width), jnp.float32),
        jnp.zeros((spaces, words_count), jnp.float32),
    )
    (totals, counts), ignored = lax.scan(block_step, start, blocks)
    return (totals, counts)


def on_device(samples, centroid_table, owner, slot, assign, codebook):
    regrouped = lax.all_to_all(samples, "narrow", split_axis=1, concat_axis=0, tiled=True)
    group_rows = regrouped.shape[0]
    owner_of = owner[assign]
    slot_of = slot[assign]
    whole = lax.all_gather(centroid_table, "wide", axis=0, tiled=True)
    centre = jnp.take(whole, owner_of * centroid_table.shape[0] + slot_of, axis=0)
    residual = (regrouped.astype(jnp.float32) - centre.astype(jnp.float32)).astype(jnp.bfloat16)
    spaces = codebook.shape[0]
    sub_width = codebook.shape[2]
    block_size = 512
    blocks = residual.reshape(group_rows // block_size, block_size, spaces, sub_width)
    codewords = codebook
    narrow_words = codebook.astype(jnp.bfloat16)
    codeword_norm_values = jnp.sum(codebook * codebook, axis=2)
    for iteration in range(ITERS):
        narrow_words = codewords.astype(jnp.bfloat16)
        codeword_norm_values = jnp.sum(codewords * codewords, axis=2)
        totals, counts = score_pass(blocks, narrow_words, codeword_norm_values)
        totals, counts = lax.psum((totals, counts), "wide")
        codewords = (totals + prior_weight * codewords) / (counts[:, :, None] + prior_weight)
    return (residual, codewords)


def solution(mesh):
    return jax.shard_map(
        on_device,
        mesh=mesh,
        in_specs=(
            P(("wide", "narrow"), None),
            P("wide", "narrow"),
            P(),
            P(),
            P("wide"),
            P("narrow", None, None),
        ),
        out_specs=(P("wide", "narrow"), P("narrow", None, None)),
        check_vma=False,
    )
```

profile of v0, /device:TPU:0, one launch (start us, length us, event | category | flops | bytes accessed | tf_op | source)
XLA Modules:
  0.0 518.3 jit_solution(10853874548214603583)
XLA Ops:
  14.5 11.8 %gather_fusion.1 = s32[2048]{0:T(1024)S(1)} fusion(s32[16384]{0:T(1024)S(1)} %copy-done, s32[2048]{0:T(1024)S(1)} %fusion.55), kind=kCustom, calls=%fused_computation.1 | custom fusion | bytes 24576 | tf_op jit(solution)/shard_map/gather | solution.py:43
  26.3 11.8 %gather_fusion = s32[2048]{0:T(1024)S(1)} fusion(s32[16384]{0:T(1024)S(1)} %copy-done.2, s32[2048]{0:T(1024)S(1)} %fusion.55), kind=kCustom, calls=%fused_computation | custom fusion | bytes 24576 | tf_op jit(solution)/shard_map/gather | solution.py:42
  44.7 92.6 %all-gather.2.cloned.1.call-done = bf16[16384,256]{1,0:T(8,128)(2,1)} async-done(((bf16[2048,256]{1,0:T(8,128)(2,1)}), bf16[16384,256]{1,0:T(8,128)(2,1)}) %all-gather.2.cloned.1.call-update) | async-done | bytes 8388624 | tf_op jit(solution)/shard_map/all_gather | solution.py:44
  137.4 11.1 %gather_fusion.2 = bf16[2048,256]{1,0:T(8,128)(2,1)S(1)} fusion(bf16[16384,256]{1,0:T(8,128)(2,1)} %all-gather.2.cloned.1.call-done, s32[2048]{0:T(1024)S(1)} %broadcast_clamp_fusion), kind=kCustom, calls=%fused_computation.2 | custom fusion | bytes 2105344 | tf_op jit(solution)/shard_map/jit(_take)/gather | solution.py:45
  158.4 69.5 %while.26 = (s32[]{:T(128)}, f32[2,2048,128]{2,1,0:T(8,128)S(1)}, f32[2,2048]{1,0:T(2,128)S(1)}, bf16[4,512,2,128]{3,1,2,0:T(8,128)(2,1)S(1)}, bf16[2,2048,128]{...) while((s32[]{:T(128)}, f32[2,2048,128]{2,1,0:T(8,128)S(1)}, ...), condition=%wide.region_5.6_spmd.clone, body=%wide.region_1.5_spmd.clone.sunk | while | flops 1093670912 | bytes 31023212 | solution.py:35
  158.4 7.2 %fusion.87 = (f32[2,512]{1,0:T(2,128)S(1)}, f32[2,512,2048]{2,1,0:T(8,128)}) fusion(f32[2,2048]{1,0:T(2,128)S(1)} %get-tuple-element.277, bf16[2,2048,128]{2,1,0:T(8,128)(2,1)} %get-tuple-element.276, bf16[4,512,2,128]{3,1,2,0:T(8,128)(2,1)S(1)} %get-tuple-element.275, s32[]{:T(128)S(6)} %copy.24), kind=kOutput, calls=%fused_computation.70.clone.1 | convolution fusion | flops 547358720 | bytes 9719812 | tf_op jit(solution)/shard_map/while/body/eval_jaxpr/sub | solution.py:25
  165.6 5.5 %convert_reduce_fusion.4 = (f32[2,2048]{1,0:T(2,128)S(1)}, bf16[2,512,2048]{2,1,0:T(8,128)(2,1)}) fusion(f32[2,512,2048]{2,1,0:T(8,128)} %get-tuple-element.242, f32[2,512]{1,0:T(2,128)S(1)} %get-tuple-element.243), kind=kLoop, calls=%fused_computation.4.clone.1 | loop fusion | flops 8384512 | bytes 12603392 | tf_op jit(solution)/shard_map/while/body/eval_jaxpr/reduce_sum | solution.py:29
  171.1 4.7 convolution_add_fusion.4
  175.8 7.2 %fusion.87 = (f32[2,512]{1,0:T(2,128)S(1)}, f32[2,512,2048]{2,1,0:T(8,128)}) fusion(f32[2,2048]{1,0:T(2,128)S(1)} %get-tuple-element.277, bf16[2,2048,128]{2,1,0:T(8,128)(2,1)} %get-tuple-element.276, bf16[4,512,2,128]{3,1,2,0:T(8,128)(2,1)S(1)} %get-tuple-element.275, s32[]{:T(128)S(6)} %copy.24), kind=kOutput, calls=%fused_computation.70.clone.1 | convolution fusion | flops 547358720 | bytes 9719812 | tf_op jit(solution)/shard_map/while/body/eval_jaxpr/sub | solution.py:25
  183.0 5.5 %convert_reduce_fusion.4 = (f32[2,2048]{1,0:T(2,128)S(1)}, bf16[2,512,2048]{2,1,0:T(8,128)(2,1)}) fusion(f32[2,512,2048]{2,1,0:T(8,128)} %get-tuple-element.242, f32[2,512]{1,0:T(2,128)S(1)} %get-tuple-element.243), kind=kLoop, calls=%fused_computation.4.clone.1 | loop fusion | flops 8384512 | bytes 12603392 | tf_op jit(solution)/shard_map/while/body/eval_jaxpr/reduce_sum | solution.py:29
  188.5 4.7 convolution_add_fusion.4
  193.2 7.2 %fusion.87 = (f32[2,512]{1,0:T(2,128)S(1)}, f32[2,512,2048]{2,1,0:T(8,128)}) fusion(f32[2,2048]{1,0:T(2,128)S(1)} %get-tuple-element.277, bf16[2,2048,128]{2,1,0:T(8,128)(2,1)} %get-tuple-element.276, bf16[4,512,2,128]{3,1,2,0:T(8,128)(2,1)S(1)} %get-tuple-element.275, s32[]{:T(128)S(6)} %copy.24), kind=kOutput, calls=%fused_computation.70.clone.1 | convolution fusion | flops 547358720 | bytes 9719812 | tf_op jit(solution)/shard_map/while/body/eval_jaxpr/sub | solution.py:25
  200.3 5.5 %convert_reduce_fusion.4 = (f32[2,2048]{1,0:T(2,128)S(1)}, bf16[2,512,2048]{2,1,0:T(8,128)(2,1)}) fusion(f32[2,512,2048]{2,1,0:T(8,128)} %get-tuple-element.242, f32[2,512]{1,0:T(2,128)S(1)} %get-tuple-element.243), kind=kLoop, calls=%fused_computation.4.clone.1 | loop fusion | flops 8384512 | bytes 12603392 | tf_op jit(solution)/shard_map/while/body/eval_jaxpr/reduce_sum | solution.py:29
  205.9 4.7 convolution_add_fusion.4
  210.6 7.2 %fusion.87 = (f32[2,512]{1,0:T(2,128)S(1)}, f32[2,512,2048]{2,1,0:T(8,128)}) fusion(f32[2,2048]{1,0:T(2,128)S(1)} %get-tuple-element.277, bf16[2,2048,128]{2,1,0:T(8,128)(2,1)} %get-tuple-element.276, bf16[4,512,2,128]{3,1,2,0:T(8,128)(2,1)S(1)} %get-tuple-element.275, s32[]{:T(128)S(6)} %copy.24), kind=kOutput, calls=%fused_computation.70.clone.1 | convolution fusion | flops 547358720 | bytes 9719812 | tf_op jit(solution)/shard_map/while/body/eval_jaxpr/sub | solution.py:25
  217.7 5.5 %convert_reduce_fusion.4 = (f32[2,2048]{1,0:T(2,128)S(1)}, bf16[2,512,2048]{2,1,0:T(8,128)(2,1)}) fusion(f32[2,512,2048]{2,1,0:T(8,128)} %get-tuple-element.242, f32[2,512]{1,0:T(2,128)S(1)} %get-tuple-element.243), kind=kLoop, calls=%fused_computation.4.clone.1 | loop fusion | flops 8384512 | bytes 12603392 | tf_op jit(solution)/shard_map/while/body/eval_jaxpr/reduce_sum | solution.py:29
  223.2 4.7 convolution_add_fusion.4
  229.4 35.4 %psum.29 = f32[2,2048]{1,0:T(2,128)S(1)} all-reduce(f32[2,2048]{1,0:T(2,128)S(1)} %get-tuple-element.69), channel_id=1, replica_groups=mesh['wide'=8,'narrow'=4] {'wide'}, use_global_device_ids=true, to_apply=%region_7.8 | all-reduce | flops 4096 | bytes 32768 | tf_op jit(solution)/shard_map/psum | solution.py:58
  264.8 65.7 %all-reduce.3.cloned.1.call-done = f32[2,2048,128]{2,1,0:T(8,128)} async-done(((f32[2,2048,128]{2,1,0:T(8,128)}), f32[2,2048,128]{2,1,0:T(8,128)}) %all-reduce.3.cloned.1.call-update) | async-done | bytes 2097168 | tf_op jit(solution)/shard_map/psum | solution.py:58
  335.8 69.5 %while.27 = (s32[]{:T(128)}, f32[2,2048,128]{2,1,0:T(8,128)S(1)}, f32[2,2048]{1,0:T(2,128)S(1)}, bf16[4,512,2,128]{3,1,2,0:T(8,128)(2,1)S(1)}, bf16[2,2048,128]{...) while((s32[]{:T(128)}, f32[2,2048,128]{2,1,0:T(8,128)S(1)}, ...), condition=%wide.region_13.14_spmd.clone, body=%wide.region_9.0_spmd.clone.sunk | while | flops 1093670912 | bytes 31023212 | solution.py:35
  335.8 7.1 %fusion.92 = (f32[2,512]{1,0:T(2,128)S(1)}, f32[2,512,2048]{2,1,0:T(8,128)}) fusion(f32[2,2048]{1,0:T(2,128)S(1)} %get-tuple-element.301, bf16[2,2048,128]{2,1,0:T(8,128)(2,1)} %get-tuple-element.300, bf16[4,512,2,128]{3,1,2,0:T(8,128)(2,1)S(1)} %get-tuple-element.299, s32[]{:T(128)S(6)} %copy.34), kind=kOutput, calls=%fused_computation.71.clone.1 | convolution fusion | flops 547358720 | bytes 9719812 | tf_op jit(solution)/shard_map/while/body/eval_jaxpr/sub | solution.py:25
  342.9 5.5 %convert_reduce_fusion.5 = (f32[2,2048]{1,0:T(2,128)S(1)}, bf16[2,512,2048]{2,1,0:T(8,128)(2,1)}) fusion(f32[2,512,2048]{2,1,0:T(8,128)} %get-tuple-element.252, f32[2,512]{1,0:T(2,128)S(1)} %get-tuple-element.253), kind=kLoop, calls=%fused_computation.28.clone.1 | loop fusion | flops 8384512 | bytes 12603392 | tf_op jit(solution)/shard_map/while/body/eval_jaxpr/reduce_sum | solution.py:29
  348.4 4.7 convolution_add_fusion.5
  353.2 7.2 %fusion.92 = (f32[2,512]{1,0:T(2,128)S(1)}, f32[2,512,2048]{2,1,0:T(8,128)}) fusion(f32[2,2048]{1,0:T(2,128)S(1)} %get-tuple-element.301, bf16[2,2048,128]{2,1,0:T(8,128)(2,1)} %get-tuple-element.300, bf16[4,512,2,128]{3,1,2,0:T(8,128)(2,1)S(1)} %get-tuple-element.299, s32[]{:T(128)S(6)} %copy.34), kind=kOutput, calls=%fused_computation.71.clone.1 | convolution fusion | flops 547358720 | bytes 9719812 | tf_op jit(solution)/shard_map/while/body/eval_jaxpr/sub | solution.py:25
  360.3 5.5 %convert_reduce_fusion.5 = (f32[2,2048]{1,0:T(2,128)S(1)}, bf16[2,512,2048]{2,1,0:T(8,128)(2,1)}) fusion(f32[2,512,2048]{2,1,0:T(8,128)} %get-tuple-element.252, f32[2,512]{1,0:T(2,128)S(1)} %get-tuple-element.253), kind=kLoop, calls=%fused_computation.28.clone.1 | loop fusion | flops 8384512 | bytes 12603392 | tf_op jit(solution)/shard_map/while/body/eval_jaxpr/reduce_sum | solution.py:29
  365.8 4.7 convolution_add_fusion.5
  370.5 7.2 %fusion.92 = (f32[2,512]{1,0:T(2,128)S(1)}, f32[2,512,2048]{2,1,0:T(8,128)}) fusion(f32[2,2048]{1,0:T(2,128)S(1)} %get-tuple-element.301, bf16[2,2048,128]{2,1,0:T(8,128)(2,1)} %get-tuple-element.300, bf16[4,512,2,128]{3,1,2,0:T(8,128)(2,1)S(1)} %get-tuple-element.299, s32[]{:T(128)S(6)} %copy.34), kind=kOutput, calls=%fused_computation.71.clone.1 | convolution fusion | flops 547358720 | bytes 9719812 | tf_op jit(solution)/shard_map/while/body/eval_jaxpr/sub | solution.py:25
  377.7 5.5 %convert_reduce_fusion.5 = (f32[2,2048]{1,0:T(2,128)S(1)}, bf16[2,512,2048]{2,1,0:T(8,128)(2,1)}) fusion(f32[2,512,2048]{2,1,0:T(8,128)} %get-tuple-element.252, f32[2,512]{1,0:T(2,128)S(1)} %get-tuple-element.253), kind=kLoop, calls=%fused_computation.28.clone.1 | loop fusion | flops 8384512 | bytes 12603392 | tf_op jit(solution)/shard_map/while/body/eval_jaxpr/reduce_sum | solution.py:29
  387.9 7.2 %fusion.92 = (f32[2,512]{1,0:T(2,128)S(1)}, f32[2,512,2048]{2,1,0:T(8,128)}) fusion(f32[2,2048]{1,0:T(2,128)S(1)} %get-tuple-element.301, bf16[2,2048,128]{2,1,0:T(8,128)(2,1)} %get-tuple-element.300, bf16[4,512,2,128]{3,1,2,0:T(8,128)(2,1)S(1)} %get-tuple-element.299, s32[]{:T(128)S(6)} %copy.34), kind=kOutput, calls=%fused_computation.71.clone.1 | convolution fusion | flops 547358720 | bytes 9719812 | tf_op jit(solution)/shard_map/while/body/eval_jaxpr/sub | solution.py:25
  395.1 5.5 %convert_reduce_fusion.5 = (f32[2,2048]{1,0:T(2,128)S(1)}, bf16[2,512,2048]{2,1,0:T(8,128)(2,1)}) fusion(f32[2,512,2048]{2,1,0:T(8,128)} %get-tuple-element.252, f32[2,512]{1,0:T(2,128)S(1)} %get-tuple-element.253), kind=kLoop, calls=%fused_computation.28.clone.1 | loop fusion | flops 8384512 | bytes 12603392 | tf_op jit(solution)/shard_map/while/body/eval_jaxpr/reduce_sum | solution.py:29
  412.3 36.7 %psum.31 = f32[2,2048]{1,0:T(2,128)S(1)} all-reduce(f32[2,2048]{1,0:T(2,128)S(1)} %get-tuple-element.71), channel_id=1, replica_groups=mesh['wide'=8,'narrow'=4] {'wide'}, use_global_device_ids=true, to_apply=%region_15.16 | all-reduce | flops 4096 | bytes 32768 | tf_op jit(solution)/shard_map/psum | solution.py:58
  449.0 59.9 %all-reduce.5.cloned.1.call-done = f32[2,2048,128]{2,1,0:T(8,128)} async-done(((f32[2,2048,128]{2,1,0:T(8,128)}), f32[2,2048,128]{2,1,0:T(8,128)}) %all-reduce.5.cloned.1.call-update) | async-done | bytes 2097168 | tf_op jit(solution)/shard_map/psum | solution.py:58
  (62 shorter events, 49.9 us)
Async XLA Ops:
  7.2 7.3 %copy-start = (s32[16384]{0:T(1024)S(1)}, s32[16384]{0:T(1024)}, u32[]{:S(2)}) copy-start(s32[16384]{0:T(1024)} %param.13) | copy-start | bytes 196612
  7.2 130.2 %all-gather.2.cloned.1.call-start = ((), (), s32[]{:S(2)}) async-start(), calls=%async_computation.1 | async-start | bytes 9437184 | tf_op jit(solution)/shard_map/all_gather | solution.py:44
  7.9 6.6 %copy-start.9 = (s32[2048]{0:T(1024)S(1)}, s32[2048]{0:T(1024)}, u32[]{:S(2)}) copy-start(s32[2048]{0:T(1024)} %param.14) | copy-start | bytes 24580
  10.2 31.9 %all-to-all-start = ((bf16[512,4,256]{0,2,1:T(8,128)(2,1)}), bf16[512,4,256]{0,2,1:T(8,128)(2,1)S(1)}, u32[]{:S(2)}, u32[]{:S(2)}) async-start(bf16[512,4,256]{0,2,1:T(8,128)(2,1)} %bitcast), calls=%async_computation | async-start | bytes 2097152 | tf_op jit(solution)/shard_map/all_to_all | solution.py:40
  14.5 316.0 %all-reduce.3.cloned.1.call-start = ((), (), s32[]{:S(2)}) async-start(), calls=%async_computation.2 | async-start | bytes 4194304 | tf_op jit(solution)/shard_map/psum | solution.py:58
  14.5 11.8 %copy-start.2 = (s32[16384]{0:T(1024)S(1)}, s32[16384]{0:T(1024)}, u32[]{:S(2)}) copy-start(s32[16384]{0:T(1024)} %param.12) | copy-start | bytes 196612
  148.5 5.1 copy-start.7
  227.9 1.3 copy-start.3
  229.3 279.6 %all-reduce.5.cloned.1.call-start = ((), (), s32[]{:S(2)}) async-start(), calls=%async_computation.3 | async-start | bytes 4194304 | tf_op jit(solution)/shard_map/psum | solution.py:58
  333.3 1.3 copy-start.5
  405.3 1.3 copy-start.4
  406.6 3.0 copy-start.8
  409.6 99.3 %copy-start.6 = (f32[2,2048,128]{2,1,0:T(8,128)S(1)}, f32[2,2048,128]{2,1,0:T(8,128)}, u32[]{:S(2)}) copy-start(f32[2,2048,128]{2,1,0:T(8,128)} %copy-done.5) | copy-start | bytes 6291460
  449.0 62.8 %copy-start.1 = (s32[16384]{0:T(1024)S(1)}, s32[16384]{0:T(1024)}, u32[]{:S(2)}) copy-start(s32[16384]{0:T(1024)} %param.13) | copy-start | bytes 196612
Sparse Core Ops, SparseCore 0:
  10.1 127.1 all-gather.1
  229.4 101.0 all-reduce.2
  406.7 102.1 all-reduce.4
where the time goes:
time: 519 us; the launch traced here: 518 us
  waiting for transfers between devices  219 us (42%)
  matrix products  94.6 us (18%)
  blocking collectives  72.1 us (14%)
  other arithmetic  63.7 us (12%)
  local copies, waits for them, and re-layouts  50.5 us (10%)
  between operations  14 us (3%)
    psum x2, waiting for transfers between devices, on_device(): totals, counts = lax.psum((totals, counts), 'wide')  126 us
    all_gather x1, waiting for transfers between devices, on_device(): whole = lax.all_gather(centroid_table, 'wide', axis=0, tiled=True)  92.6 us
    psum x2, blocking collectives, on_device(): totals, counts = lax.psum((totals, counts), 'wide')  72.1 us
    sub x8, matrix products, block_step(): weights_soft = jax.nn.softmax(score_matrix, axis=2).astype(jnp.bfloat16)  57.2 us
    reduce_sum x8, other arithmetic, block_step(): jnp.sum(weights_soft, axis=1, dtype=jnp.float32)  44.1 us
    dot_general x8, matrix products, block_step(): jnp.einsum('mbk,bms->mks', weights_soft, row_block, preferred_element_typ...  37.4 us
    gather x3, local copies, waits for them, and re-layouts, on_device(): jnp.take(whole, owner_of * centroid_table.shape[0] + slot_of, axis=0)  16.1 us
    gather x1, local copies, waits for them, and re-layouts, on_device(): slot_of = slot[assign]  11.8 us
  transfers between devices with their start and end apart: 4, of which 3 were waited for; matrix products, arithmetic and copies ran while one was open for 7% of the time, Pallas kernels for 0%

commit v1 on v0

v1 whole, which is shorter than its diff:
```python
import functools

import jax
import jax.numpy as jnp
from jax import lax
from jax.experimental import pallas as pl
from jax.experimental.pallas import tpu as pltpu
from jax.sharding import PartitionSpec as P

ITERS = 2
SOFTNESS = 16.0
PRIOR = 1.0
LANES = 128
LOG2E = 1.4426950408889634
TINY = 2.0**-64

f32 = jnp.float32
bf16 = jnp.bfloat16
i32 = jnp.int32

NN = (((1,), (0,)), ((), ()))
NT = (((1,), (1,)), ((), ()))


def mm(a, b, dims=NN):
    return lax.dot_general(a, b, dims, preferred_element_type=f32)


def iota(shape, dim):
    return lax.broadcasted_iota(i32, shape, dim)


def onehot(mask):
    return jnp.where(mask, 1.0, 0.0).astype(bf16)


def pad_rows(x, rows):
    if x.shape[0] == rows:
        return x
    return jnp.concatenate([x, jnp.zeros((rows - x.shape[0],) + x.shape[1:], x.dtype)], axis=0)


def pieces(v):
    high = v.astype(bf16).astype(f32)
    rest = v - high
    middle = rest.astype(bf16).astype(f32)
    return high, middle, rest - middle


def call(body, out_shape, scratch=(), in_specs=None, name=None, prefetch=0):
    return pl.pallas_call(
        body,
        out_shape=out_shape,
        grid_spec=pltpu.PrefetchScalarGridSpec(
            num_scalar_prefetch=prefetch,
            grid=(1,),
            in_specs=in_specs,
            out_specs=jax.tree.map(
                lambda s: pl.BlockSpec(s.shape, lambda i, *_, n=len(s.shape): (0,) * n), out_shape
            ),
            scratch_shapes=scratch,
        ),
        compiler_params=pltpu.CompilerParams(vmem_limit_bytes=56 * 1024 * 1024),
        name=name,
    )


def whole(x):
    return pl.BlockSpec(x.shape, lambda i, *_, n=len(x.shape): (0,) * n)


def lookup_kernel(wide, cap, assign_ref, owner_ref, slot_ref, req_ref, own_ref, rank_ref, hot, looked, stack, weighted, ranked):
    blocks = assign_ref.shape[0]
    high_count = owner_ref.shape[0]
    group = stack.shape[0] // blocks
    assign = assign_ref[...]
    high = assign >> 7
    low = assign & (LANES - 1)
    sub_high = iota((high_count, LANES), 0)
    for c in range(blocks):
        hot[:, c * LANES : (c + 1) * LANES] = onehot(sub_high == high[c : c + 1, :])
    slots = slot_ref[...]
    table = jnp.concatenate(
        [t.astype(f32).T for t in (owner_ref[...], slots >> 8, slots & 255)], axis=0
    ).astype(bf16)
    looked[...] = mm(table, hot[...])
    sub = iota((LANES, LANES), 0)
    sub_group = iota((group, LANES), 0).astype(f32)
    for c in range(blocks):
        lanes = slice(c * LANES, (c + 1) * LANES)
        pick = sub == low[c : c + 1, :]
        values = [
            jnp.sum(jnp.where(pick, looked[p * LANES : (p + 1) * LANES, lanes], 0.0), axis=0, keepdims=True)
            for p in range(3)
        ]
        mine = jnp.where(sub_group == values[0], 1.0, 0.0)
        own_ref[c : c + 1, :] = values[0].astype(i32)
        stack[c * group : (c + 1) * group, :] = mine.astype(bf16)
        weighted[0:group, lanes] = (mine * values[1]).astype(bf16)
        weighted[group : 2 * group, lanes] = (mine * values[2]).astype(bf16)
    before = onehot(iota((LANES, LANES), 0) < iota((LANES, LANES), 1))
    inside = mm(stack[...], before)
    count = mm(stack[...], jnp.ones((LANES, LANES), bf16))
    offset = jnp.zeros((group, LANES), f32)
    sub_cap = iota((cap, LANES), 0).astype(f32)
    for c in range(blocks):
        rows = slice(c * group, (c + 1) * group)
        mine = stack[rows, :].astype(f32)
        rank = jnp.sum(mine * (inside[rows, :] + offset), axis=0, keepdims=True)
        offset = offset + count[rows, :]
        rank_ref[c : c + 1, :] = rank.astype(i32)
        ranked[:, c * LANES : (c + 1) * LANES] = onehot(sub_cap == rank)
    found = mm(weighted[...], ranked[...], NT)
    req_ref[...] = (found[0:wide] * 256.0 + found[group : group + wide]).astype(i32)


def lookup(assign, owner, slot, wide, cap):
    rows = assign.shape[0]
    blocks = rows // LANES
    high_count = owner.shape[0] // LANES
    group = max(wide, 16)
    args = (
        assign.reshape(blocks, LANES),
        owner.reshape(high_count, LANES),
        slot.reshape(high_count, LANES),
    )
    return call(
        functools.partial(lookup_kernel, wide, cap),
        (
            jax.ShapeDtypeStruct((wide, cap), i32),
            jax.ShapeDtypeStruct((blocks, LANES), i32),
            jax.ShapeDtypeStruct((blocks, LANES), i32),
        ),
        scratch=[
            pltpu.VMEM((high_count, rows), bf16),
            pltpu.VMEM((3 * LANES, rows), f32),
            pltpu.VMEM((blocks * group, LANES), bf16),
            pltpu.VMEM((2 * group, rows), bf16),
            pltpu.VMEM((cap, rows), bf16),
        ],
        in_specs=[whole(a) for a in args],
        name="lookup",
    )(*args)


def pick_kernel(spaces, step, req_ref, table_ref, *outs):
    wide, cap = req_ref.shape
    slots = table_ref.shape[0]
    req = pad_rows(req_ref[...], LANES)
    shift = step.bit_length() - 1
    high_t = (req >> shift).astype(f32).T
    low_t = (req & (step - 1)).astype(f32).T
    lane = iota((cap, step), 1).astype(f32)
    for d in range(wide):
        hot = onehot(lane == low_t[:, d : d + 1])
        high = high_t[:, d : d + 1]
        rows = mm(hot, table_ref[0:step, :])
        for h in range(1, slots // step):
            rows = jnp.where(high == float(h), mm(hot, table_ref[h * step : (h + 1) * step, :]), rows)
        for i in range(spaces):
            block = (d % spaces + 1 + i) % spaces
            outs[i][d] = rows[:, block * LANES : (block + 1) * LANES].astype(bf16)


def pick(req, table, spaces):
    wide, cap = req.shape
    return call(
        functools.partial(pick_kernel, spaces, min(512, table.shape[0])),
        tuple(jax.ShapeDtypeStruct((wide, cap, LANES), bf16) for _ in range(spaces)),
        in_specs=[whole(req), whole(table)],
        name="pick",
    )(req, table)


def place_kernel(wide, where_ref, own_ref, rank_ref, sample_ref, *refs):
    bufs, (res_ref, res_t_ref) = refs[:wide], refs[wide:]
    rows = sample_ref.shape[0]
    cap = bufs[0].shape[0]
    me = where_ref[0]
    own_t = pad_rows(own_ref[...], LANES).astype(f32).T
    rank_t = pad_rows(rank_ref[...], LANES).astype(f32).T
    lane = iota((LANES, cap), 1).astype(f32)
    for b in range(rows // LANES):
        hot = onehot(lane == rank_t[:, b : b + 1])
        owner = own_t[:, b : b + 1]
        total = jnp.zeros((LANES, LANES), f32)
        for k in range(0, wide, 2):
            pair = mm(hot, jnp.concatenate([bufs[k][...], bufs[k + 1][...]], axis=1))
            for t in range(2):
                source = (me ^ (k + t)).astype(f32)
                total = jnp.where(owner == source, pair[:, t * LANES : (t + 1) * LANES], total)
        part = slice(b * LANES, (b + 1) * LANES)
        res = (sample_ref[part, :].astype(f32) - total).astype(bf16)
        res_ref[part, :] = res
        res_t_ref[:, part] = res.astype(f32).T.astype(bf16)


def place(me, column, own, rank, samples, bufs):
    wide = len(bufs)
    rows = samples.shape[0]
    where = jnp.stack([me, column]).astype(i32)
    return call(
        functools.partial(place_kernel, wide),
        (
            jax.ShapeDtypeStruct((rows, LANES), bf16),
            jax.ShapeDtypeStruct((LANES, rows), bf16),
        ),
        in_specs=[whole(own), whole(rank), pl.BlockSpec((rows, LANES), lambda i, w: (0, w[1]))]
        + [whole(b) for b in bufs],
        name="place",
        prefetch=1,
    )(where, own, rank, samples, *bufs)


def words_block(words, norm_columns):
    rows = words.shape[0]
    lane = iota((rows, LANES), 1)
    extra = jnp.where((lane >= 3) & (lane < 6), 1.0, 0.0)
    for p in range(3):
        extra = jnp.where(lane == p, norm_columns[p], extra)
    return jnp.concatenate([words * (2.0 / SOFTNESS), extra], axis=1).astype(bf16)


def first_words_kernel(where_ref, code_ref, words_ref):
    count = code_ref.shape[1]
    step = min(256, count)
    for b in range(count // step):
        part = slice(b * step, (b + 1) * step)
        code = code_ref[0, part, :]
        norm = jnp.sum(code * code, axis=1, keepdims=True) * (-1.0 / SOFTNESS)
        words_ref[part, :] = words_block(code.astype(bf16).astype(f32), pieces(norm))


def first_words(space, codebook):
    _, count, width = codebook.shape
    return call(
        first_words_kernel,
        jax.ShapeDtypeStruct((count, 2 * LANES), bf16),
        in_specs=[pl.BlockSpec((1, count, width), lambda i, w: (w[0], 0, 0))],
        name="first_words",
        prefetch=1,
    )(space.reshape(1).astype(i32), codebook)


def next_words_kernel(shard, where_ref, *refs):
    messages, words_ref = refs[:-1], refs[-1]
    q = where_ref[0]
    size = min(shard, LANES)
    per = shard // size
    for k, ref in enumerate(messages):
        norm_t = pad_rows(ref[shard:, :].astype(f32), LANES).T
        first = (q ^ k) * shard
        for a in range(per):
            columns = [norm_t[0:size, p * per + a : p * per + a + 1] for p in range(3)]
            words = ref[a * size : (a + 1) * size, :].astype(f32)
            start = pl.multiple_of(first + a * size, size)
            words_ref[pl.ds(start, size), :] = words_block(words, columns)


def next_words(q, messages, shard):
    return call(
        functools.partial(next_words_kernel, shard),
        jax.ShapeDtypeStruct((shard * len(messages), 2 * LANES), bf16),
        in_specs=[whole(m) for m in messages],
        name="next_words",
        prefetch=1,
    )(q.reshape(1).astype(i32), *messages)


def pass_kernel(parts, shards, block, words_ref, *refs):
    inputs, out_ref, aug, soft, scaled, least = refs[:parts], *refs[parts:]
    words = words_ref.shape[0]
    rows = inputs[0].shape[1]
    step = min(256, words)
    sub = iota((16, block), 0)
    sub_wide = iota((LANES, block), 0)

    def softmax_block(b, slow):
        lanes = pl.ds(pl.multiple_of(b * block, block), block)
        points = aug[:, lanes]

        def scores(c):
            return mm(words_ref[c * step : (c + 1) * step, :], points)

        top = None
        if slow:
            for c in range(words // step):
                now = jnp.max(scores(c), axis=0, keepdims=True)
                top = now if top is None else jnp.maximum(top, now)
        total = jnp.zeros((8, block), f32)
        for c in range(words // step):
            s = scores(c)
            if slow:
                s = s - top
            e = jnp.exp2(s * LOG2E)
            total = total + jnp.sum(e.reshape(step // 8, 8, block), axis=0)
            soft[c * step : (c + 1) * step, lanes] = e.astype(bf16)
        total = jnp.sum(total, axis=0, keepdims=True)
        inverse = 1.0 / total
        x = points[0:LANES, :].astype(f32)
        high = inverse.astype(bf16).astype(f32)
        tail = jnp.where(sub_wide == 0, high, jnp.where(sub_wide == 1, inverse - high, 0.0))
        both = jnp.concatenate([x * inverse, tail], axis=0)
        scaled[lanes, :] = both.T.astype(bf16)
        return total

    for n, ref in enumerate(inputs):
        for b in range(rows // block):
            part = slice(b * block, (b + 1) * block)
            lanes = slice(n * rows + b * block, n * rows + (b + 1) * block)
            x = ref[:, part]
            wide_x = x.astype(f32)
            norm = jnp.sum(wide_x * wide_x, axis=0, keepdims=True) * (-1.0 / SOFTNESS)
            head = jnp.where(sub < 3, 1.0, 0.0)
            for p, piece in enumerate(pieces(norm)):
                head = jnp.where(sub == 3 + p, piece, head)
            aug[0:LANES, lanes] = x
            aug[LANES : LANES + 16, lanes] = head.astype(bf16)
            aug[LANES + 16 :, lanes] = jnp.zeros((LANES - 16, block), bf16)
    count = parts * rows // block
    least[...] = jnp.full(least.shape, 1.0, f32)

    def fast(b, carry):
        total = softmax_block(b, False)
        least[...] = jnp.minimum(least[...], total)
        return carry

    lax.fori_loop(0, count, fast, 0)

    @pl.when(jnp.min(least[...]) < TINY)
    def _():
        def exact(b, carry):
            softmax_block(b, True)
            return carry

        lax.fori_loop(0, count, exact, 0)

    shard = words // shards
    size = min(shard, LANES)
    per = shard // size
    extra = out_ref.shape[1] - shard
    lane_row = iota((extra, LANES), 0)
    for j in range(shards):
        tail = jnp.zeros((extra, LANES), f32)
        sums = mm(soft[j * shard : (j + 1) * shard, :], scaled[...])
        out_ref[j, 0:shard, :] = sums[:, 0:LANES].astype(bf16)
        for a in range(per):
            turned = pad_rows(sums[a * size : (a + 1) * size, LANES:], LANES).T
            counts = turned[0:1, :] + turned[1:2, :]
            high = counts.astype(bf16).astype(f32)
            tail = jnp.where(lane_row == a, high, tail)
            tail = jnp.where(lane_row == per + a, counts - high, tail)
        out_ref[j, shard:, :] = tail.astype(bf16)


def em_pass(words, inputs, shards, extra):
    count = words.shape[0]
    rows = inputs[0].shape[1]
    every = rows * len(inputs)
    block = min(256, rows)
    return call(
        functools.partial(pass_kernel, len(inputs), shards, block),
        jax.ShapeDtypeStruct((shards, count // shards + extra, LANES), bf16),
        scratch=[
            pltpu.VMEM((2 * LANES, every), bf16),
            pltpu.VMEM((count, every), bf16),
            pltpu.VMEM((every, 2 * LANES), bf16),
            pltpu.VMEM((1, block), f32),
        ],
        in_specs=[whole(words)] + [whole(x) for x in inputs],
        name="em_pass",
    )(words, *inputs)


def update_kernel(shard, code_ref, *refs):
    messages, (new_ref, out_ref) = refs[:-2], refs[-2:]
    size = min(shard, LANES)
    per = shard // size
    total = jnp.zeros(messages[0].shape, f32)
    for ref in messages:
        total = total + ref[...].astype(f32)
    tail = total[shard:, :]
    counts_t = pad_rows(tail[0:per] + tail[per : 2 * per], LANES).T
    row = iota(tail.shape, 0)
    lane = iota((LANES, LANES), 1)
    norms = jnp.zeros(tail.shape, f32)
    for a in range(per):
        part = slice(a * size, (a + 1) * size)
        new = (total[part, :] + PRIOR * code_ref[part, :]) / (counts_t[0:size, a : a + 1] + PRIOR)
        new_ref[part, :] = new
        out_ref[part, :] = new.astype(bf16)
        norm = pad_rows(jnp.sum(new * new, axis=1, keepdims=True) * (-1.0 / SOFTNESS), LANES)
        columns = jnp.zeros((LANES, LANES), f32)
        for p, piece in enumerate(pieces(norm)):
            columns = jnp.where(lane == p, piece, columns)
        turned = columns.T
        for p in range(3):
            norms = jnp.where(row == p * per + a, turned[p : p + 1, :], norms)
    out_ref[shard:, :] = norms.astype(bf16)


def update(code, messages):
    shard = code.shape[0]
    return call(
        functools.partial(update_kernel, shard),
        (
            jax.ShapeDtypeStruct(code.shape, f32),
            jax.ShapeDtypeStruct(messages[0].shape, bf16),
        ),
        in_specs=[whole(code)] + [whole(m) for m in messages],
        name="update",
    )(code, *messages)


def finish_kernel(shards, where_ref, *refs):
    messages, out_ref = refs[:-1], refs[-1]
    spaces, words, _ = out_ref.shape
    shard = words // shards
    q, s = where_ref[0], where_ref[1]
    for t in range(spaces):
        space = lax.rem(s - t + spaces, spaces)
        for k in range(shards):
            start = pl.multiple_of((q ^ k) * shard, shard)
            out_ref[space, pl.ds(start, shard), :] = messages[t * shards + k][0:shard, :].astype(f32)


def finish(q, s, messages, shape, shards):
    return call(
        functools.partial(finish_kernel, shards),
        jax.ShapeDtypeStruct(shape, f32),
        in_specs=[whole(m) for m in messages],
        name="finish",
        prefetch=1,
    )(jnp.stack([q, s]).astype(i32), *messages)


def on_device(wide, samples, centroid_table, owner, slot, assign, codebook):
    spaces, words, sub_width = codebook.shape
    group_rows = assign.shape[0]
    cap = 2 * group_rows // wide
    shards = wide // spaces
    shard = words // shards
    per = max(1, shard // LANES)
    extra = -(-3 * per // 16) * 16
    me = lax.axis_index("wide")
    q, s = me // spaces, me % spaces

    def swap(x, k):
        return lax.ppermute(x, "wide", [(j, j ^ k) for j in range(wide)])

    def swap_shard(x, k):
        return lax.ppermute(x, "wide", [(j, j ^ (k * spaces)) for j in range(wide)])

    def turn(x, t):
        pairs = [(j, (j // spaces) * spaces + (j + t) % spaces) for j in range(wide)]
        return lax.ppermute(x, "wide", pairs)

    req, own, rank = lookup(assign, owner, slot, wide, cap)
    regrouped = lax.all_to_all(samples, "narrow", split_axis=1, concat_axis=0, tiled=True)
    asked = lax.all_to_all(req, "wide", 0, 0, tiled=True)
    chunks = pick(asked, centroid_table, spaces)
    moved = []
    for chunk in chunks:
        bufs = [lax.dynamic_index_in_dim(chunk, me, 0, keepdims=False)]
        for k in range(1, wide):
            bufs.append(swap(lax.dynamic_index_in_dim(chunk, me ^ k, 0, keepdims=False), k))
        moved.append(bufs)
    residuals, inputs = [], []
    for i in range(spaces):
        res, res_t = place(me, (s + 1 + i) % spaces, own, rank, regrouped, moved[i])
        residuals.append(res)
        inputs.append(res_t if i == spaces - 1 else turn(res_t, 1 + i))
    stacked = jnp.stack(residuals)
    residual = jnp.concatenate(
        [
            lax.dynamic_index_in_dim(stacked, (c - s - 1 + 2 * spaces) % spaces, 0, keepdims=False)
            for c in range(spaces)
        ],
        axis=1,
    )

    words_aug = first_words(s, codebook)
    mine = lax.dynamic_slice(codebook, (s, q * shard, 0), (1, shard, sub_width))[0]
    for iteration in range(ITERS):
        sums = em_pass(words_aug, inputs, shards, extra)
        parts = [lax.dynamic_index_in_dim(sums, q, 0, keepdims=False)]
        for k in range(1, shards):
            parts.append(swap_shard(lax.dynamic_index_in_dim(sums, q ^ k, 0, keepdims=False), k))
        mine, message = update(mine, parts)
        if iteration < ITERS - 1:
            got = [message] + [swap_shard(message, k) for k in range(1, shards)]
            words_aug = next_words(q, got, shard)
    message = message[0:shard]
    got = [message] + [swap_shard(message, k) for k in range(1, shards)]
    for t in range(1, spaces):
        got = got + [turn(m, t) for m in got[0:shards]]
    refined = finish(q, s, got, codebook.shape, shards)
    return (residual, refined)


def solution(mesh):
    wide = mesh.shape["wide"]
    return jax.shard_map(
        functools.partial(on_device, wide),
        mesh=mesh,
        in_specs=(
            P(("wide", "narrow"), None),
            P("wide", "narrow"),
            P(),
            P(),
            P("wide"),
            P("narrow", None, None),
        ),
        out_specs=(P("wide", "narrow"), P("narrow", None, None)),
        check_vma=False,
    )
```

time: 519 us -> 258 us (0.50)
  waiting for transfers between devices: 219 us -> 69.9 us
  Pallas kernels: 0 us -> 102 us
  matrix products: 94.6 us -> 0 us
  blocking collectives: 72.1 us -> 0 us
  other arithmetic: 63.7 us -> 2.78 us
  starting transfers between devices: 4.35 us -> 63.9 us
  local copies, waits for them, and re-layouts: 50.5 us -> 18.5 us
  between operations: 14 us -> 0.94 us
    psum x2 -> x0, waiting for transfers between devices: 126 us -> none  [on_device(): totals, counts = lax.psum((totals, counts), 'wide')]
    pallas_call x0 -> x11, Pallas kernels: none -> 102 us  [the longest x2 64.2 us: em_pass(): call(functools.partial(pass_kernel, len(inputs), shards, block), jax.Shap...]
    all_gather x1 -> x0, waiting for transfers between devices: 92.6 us -> none  [on_device(): whole = lax.all_gather(centroid_table, 'wide', axis=0, tiled=True)]
    psum x2 -> x0, blocking collectives: 72.1 us -> none  [on_device(): totals, counts = lax.psum((totals, counts), 'wide')]
    ppermute x0 -> x31, waiting for transfers between devices: none -> 65.6 us  [the longest x12 36 us: swap_shard(): return lax.ppermute(x, 'wide', [(j, j ^ k * spaces) for j in range(wide)])]
    sub x8 -> x0, matrix products: 57.2 us -> none  [block_step(): weights_soft = jax.nn.softmax(score_matrix, axis=2).astype(jnp.bfloat16)]
    ppermute x0 -> x31, starting transfers between devices: none -> 53.1 us  [the longest x14 29.2 us: swap(): return lax.ppermute(x, 'wide', [(j, j ^ k) for j in range(wide)])]
    reduce_sum x10 -> x0, other arithmetic: 50.9 us -> none  [the longest x8 44.1 us: block_step(): jnp.sum(weights_soft, axis=1, dtype=jnp.float32)]
  transfers between devices with their start and end apart: 4 -> 33, of which waited for: 3 -> 15; matrix products, arithmetic and copies ran while one was open for 7% -> 4% of each run, Pallas kernels for 0% -> 7%
where the time goes in v1:
time: 258 us
  Pallas kernels  102 us (40%)
  waiting for transfers between devices  69.9 us (27%)
  starting transfers between devices  63.9 us (25%)
  local copies, waits for them, and re-layouts  18.5 us (7%)
  other arithmetic  2.78 us (1%)
    pallas_call x2, Pallas kernels, em_pass(): call(functools.partial(pass_kernel, len(inputs), shards, block), jax.Shap...  64.2 us
    ppermute x12, waiting for transfers between devices, swap_shard(): return lax.ppermute(x, 'wide', [(j, j ^ k * spaces) for j in range(wide)])  36 us
    ppermute x14, starting transfers between devices, swap(): return lax.ppermute(x, 'wide', [(j, j ^ k) for j in range(wide)])  29.2 us
    ppermute x14, waiting for transfers between devices, swap(): return lax.ppermute(x, 'wide', [(j, j ^ k) for j in range(wide)])  26.4 us
    ppermute x12, starting transfers between devices, swap_shard(): return lax.ppermute(x, 'wide', [(j, j ^ k * spaces) for j in range(wide)])  19.8 us
    pallas_call x2, Pallas kernels, place(): call(functools.partial(place_kernel, wide), (jax.ShapeDtypeStruct((rows,...  13.2 us
    pallas_call x1, Pallas kernels, pick(): call(functools.partial(pick_kernel, spaces, min(512, table.shape[0])), tu...  7.45 us
    all_to_all x1, starting transfers between devices, on_device(): asked = lax.all_to_all(req, 'wide', 0, 0, tiled=True)  7.28 us
  transfers between devices with their start and end apart: 33, of which 15 were waited for; matrix products, arithmetic and copies ran while one was open for 4% of the time, Pallas kernels for 7%

profile of v1, /device:TPU:0, one launch (start us, length us, event | category | flops | bytes accessed | tf_op | source)
XLA Modules:
  0.0 257.7 jit_solution(883343502144100001)
XLA Ops:
  0.6 3.1 %lookup.1 = (s32[8,512]{1,0:T(8,128)}, s32[16,128]{1,0:T(8,128)}, s32[16,128]{1,0:T(8,128)}) custom-call(s32[16,128]{1,0:T(8,128)} %bitcast.84, s32[128,128]{1,0:T(8,128)} %bitcast.81, s32[128,128]{1,0:T(8,128)} %bitcast.82), custom_call_target="tpu_custom_call" | custom-call | tf_op jit(solution)/shard_map/lookup/pallas_call | solution.py:127
  5.1 7.3 %all-to-all-start.1 = ((s32[8,1,512]{2,1,0:T(1,128)}), s32[8,1,512]{2,1,0:T(1,128)S(1)}, u32[]{:S(2)}, u32[]{:S(2)}) async-start(s32[8,1,512]{2,1,0:T(1,128)} %copy.10), calls=%async_computation.1 | async-start | bytes 32768 | tf_op jit(solution)/shard_map/all_to_all | solution.py:460
  12.4 2.3 copy.15
  14.7 4.3 %all-to-all-done.1 = s32[8,1,512]{2,1,0:T(1,128)S(1)} async-done(((s32[8,1,512]{2,1,0:T(1,128)}), s32[8,1,512]{2,1,0:T(1,128)S(1)}, u32[]{:S(2)}, u32[]{:S(2)}) %all-to-all-start.1) | async-done | bytes 16416 | tf_op jit(solution)/shard_map/all_to_all | solution.py:460
  19.0 3.5 %all-to-all-start = ((bf16[512,4,256]{2,0,1:T(8,128)(2,1)}), bf16[512,4,256]{2,0,1:T(8,128)(2,1)S(1)}, u32[]{:S(2)}, u32[]{:S(2)}) async-start(bf16[512,4,256]{2,0,1:T(8,128)(2,1)} %bitcast.73), calls=%async_computation | async-start | bytes 2097152 | tf_op jit(solution)/shard_map/all_to_all | solution.py:459
  23.1 7.5 %pick.1 = (bf16[8,512,128]{2,1,0:T(8,128)(2,1)}, bf16[8,512,128]{2,1,0:T(8,128)(2,1)}) custom-call(s32[8,512]{1,0:T(8,128)} %bitcast.80, bf16[2048,256]{1,0:T(8,128)(2,1)} %table_ref.1), custom_call_target="tpu_custom_call" | custom-call | tf_op jit(solution)/shard_map/pick/pallas_call | solution.py:167
  30.6 2.1 dynamic-slice_bitcast_fusion.17
  33.8 2.4 collective-permute-start.2
  36.7 2.4 collective-permute-start.4
  41.3 4.3 %collective-permute-start.6 = (bf16[512,128]{1,0:T(8,128)(2,1)S(1)}, bf16[512,128]{1,0:T(8,128)(2,1)}, u32[]{:S(2)}, u32[]{:S(2)}) collective-permute-start(bf16[512,128]{1,0:T(8,128)(2,1)S(1)} %get-tuple-element.36), channel_id=1, source_target_pairs={{0,28},{4,24},{8,20},{12,16},{16,12},{20,8},{24,4},{28,0},{1,29},{... | collective-permute-start | bytes 393224 | tf_op jit(solution)/shard_map/ppermute | solution.py:449
  46.3 8.4 %collective-permute-done.3.refs_4_ = bf16[512,128]{1,0:T(8,128)(2,1)S(1)} collective-permute-done((bf16[512,128]{1,0:T(8,128)(2,1)S(1)}, bf16[512,128]{1,0:T(8,128)(2,1)S(1)}, u32[]{:S(2)}, u32[]{:S(2)}) %collective-permute-start.3) | collective-permute-done | bytes 131104 | tf_op jit(solution)/shard_map/ppermute | solution.py:449
  54.7 2.8 %collective-permute-done.4.refs_5_ = bf16[512,128]{1,0:T(8,128)(2,1)S(1)} collective-permute-done((bf16[512,128]{1,0:T(8,128)(2,1)S(1)}, bf16[512,128]{1,0:T(8,128)(2,1)S(1)}, u32[]{:S(2)}, u32[]{:S(2)}) %collective-permute-start.4) | collective-permute-done | bytes 131104 | tf_op jit(solution)/shard_map/ppermute | solution.py:449
  58.5 6.5 %place.2 = (bf16[2048,128]{1,0:T(8,128)(2,1)}, bf16[128,2048]{1,0:T(8,128)(2,1)}) custom-call(s32[2]{0:T(128)} %get-tuple-element.52.where_ref, s32[16,128]{1,0:T(8,128)} %get-tuple-element.14.own_ref, s32[16,128]{1,0:T(8,128)} %get-tuple-element.15.rank_ref, bf16[2048,256]{1,0:T(8,128)(2,1)} %bitcast.75, bf16[512,128]{1,0:T(8,128)(2,1)} %get-tuple-element.43.refs_0_, ...), custom_call_target="tpu_custom_call" | custom-call | tf_op jit(solution)/shard_map/place/pallas_call | solution.py:202
  67.8 4.9 %collective-permute-start.8 = (bf16[512,128]{1,0:T(8,128)(2,1)S(1)}, bf16[512,128]{1,0:T(8,128)(2,1)S(1)}, u32[]{:S(2)}, u32[]{:S(2)}) collective-permute-start(bf16[512,128]{1,0:T(8,128)(2,1)S(1)} %get-tuple-element.33), channel_id=1, source_target_pairs={{0,8},{4,12},{8,0},{12,4},{16,24},{20,28},{24,16},{28,20},{1,9},{5... | collective-permute-start | bytes 393224 | tf_op jit(solution)/shard_map/ppermute | solution.py:449
  74.7 7.4 %collective-permute-done.7.refs_1_ = bf16[512,128]{1,0:T(8,128)(2,1)S(1)} collective-permute-done((bf16[512,128]{1,0:T(8,128)(2,1)S(1)}, bf16[512,128]{1,0:T(8,128)(2,1)S(1)}, u32[]{:S(2)}, u32[]{:S(2)}) %collective-permute-start.7) | collective-permute-done | bytes 131104 | tf_op jit(solution)/shard_map/ppermute | solution.py:449
  82.1 6.8 %collective-permute-start.11 = (bf16[512,128]{1,0:T(8,128)(2,1)S(1)}, bf16[512,128]{1,0:T(8,128)(2,1)S(1)}, u32[]{:S(2)}, u32[]{:S(2)}) collective-permute-start(bf16[512,128]{1,0:T(8,128)(2,1)S(1)} %get-tuple-element.30), channel_id=1, source_target_pairs={{0,20},{4,16},{8,28},{12,24},{16,4},{20,0},{24,12},{28,8},{1,21},{... | collective-permute-start | bytes 393224 | tf_op jit(solution)/shard_map/ppermute | solution.py:449
  88.9 2.7 %collective-permute-start.12 = (bf16[512,128]{1,0:T(8,128)(2,1)S(1)}, bf16[512,128]{1,0:T(8,128)(2,1)S(1)}, u32[]{:S(2)}, u32[]{:S(2)}) collective-permute-start(bf16[512,128]{1,0:T(8,128)(2,1)S(1)} %get-tuple-element.29), channel_id=1, source_target_pairs={{0,24},{4,28},{8,16},{12,20},{16,8},{20,12},{24,0},{28,4},{1,25},{... | collective-permute-start | bytes 393224 | tf_op jit(solution)/shard_map/ppermute | solution.py:449
  92.5 2.7 %first_words.1.words_ref = bf16[2048,256]{1,0:T(8,128)(2,1)} custom-call(s32[1]{0:T(128)} %bitcast.31.where_ref, f32[2,2048,128]{2,1,0:T(8,128)} %code_ref.1), custom_call_target="tpu_custom_call" | custom-call | tf_op jit(solution)/shard_map/first_words/pallas_call | solution.py:236
  95.1 6.2 %collective-permute-done.11.refs_5_ = bf16[512,128]{1,0:T(8,128)(2,1)S(1)} collective-permute-done((bf16[512,128]{1,0:T(8,128)(2,1)S(1)}, bf16[512,128]{1,0:T(8,128)(2,1)S(1)}, u32[]{:S(2)}, u32[]{:S(2)}) %collective-permute-start.11) | collective-permute-done | bytes 131104 | tf_op jit(solution)/shard_map/ppermute | solution.py:449
  102.1 6.7 %place.3 = (bf16[2048,128]{1,0:T(8,128)(2,1)}, bf16[128,2048]{1,0:T(8,128)(2,1)}) custom-call(s32[2]{0:T(128)} %get-tuple-element.53.where_ref, s32[16,128]{1,0:T(8,128)} %get-tuple-element.14.own_ref, s32[16,128]{1,0:T(8,128)} %get-tuple-element.15.rank_ref, bf16[2048,256]{1,0:T(8,128)(2,1)} %bitcast.76, bf16[512,128]{1,0:T(8,128)(2,1)} %get-tuple-element.35.refs_0_, ...), custom_call_target="tpu_custom_call" | custom-call | tf_op jit(solution)/shard_map/place/pallas_call | solution.py:202
  109.6 31.9 %em_pass.2 = bf16[4,528,128]{2,1,0:T(8,128)(2,1)} custom-call(bf16[2048,256]{1,0:T(8,128)(2,1)} %first_words.1.words_ref, bf16[128,2048]{1,0:T(8,128)(2,1)} %copy-done.1, bf16[128,2048]{1,0:T(8,128)(2,1)} %get-tuple-element.22.refs_1_), custom_call_target="tpu_custom_call" | custom-call | tf_op jit(solution)/shard_map/em_pass/pallas_call | solution.py:361
  143.4 4.2 %collective-permute-start.15 = (bf16[528,128]{1,0:T(8,128)(2,1)S(1)}, bf16[528,128]{1,0:T(8,128)(2,1)S(1)}, u32[]{:S(2)}, u32[]{:S(2)}) collective-permute-start(bf16[528,128]{1,0:T(8,128)(2,1)S(1)} %get-tuple-element.50), channel_id=1, source_target_pairs={{0,8},{4,12},{8,0},{12,4},{16,24},{20,28},{24,16},{28,20},{1,9},{5... | collective-permute-start | bytes 405512 | tf_op jit(solution)/shard_map/ppermute | solution.py:452
  151.6 7.6 %collective-permute-done.16.refs_2_ = bf16[528,128]{1,0:T(8,128)(2,1)S(1)} collective-permute-done((bf16[528,128]{1,0:T(8,128)(2,1)S(1)}, bf16[528,128]{1,0:T(8,128)(2,1)S(1)}, u32[]{:S(2)}, u32[]{:S(2)}) %collective-permute-start.16) | collective-permute-done | bytes 135200 | tf_op jit(solution)/shard_map/ppermute | solution.py:452
  159.9 2.5 update.2
  166.7 2.3 collective-permute-done.18.refs_1_
  169.0 8.0 %collective-permute-done.19.refs_2_ = bf16[528,128]{1,0:T(8,128)(2,1)S(1)} collective-permute-done((bf16[528,128]{1,0:T(8,128)(2,1)}, bf16[528,128]{1,0:T(8,128)(2,1)S(1)}, u32[]{:S(2)}, u32[]{:S(2)}) %collective-permute-start.19) | collective-permute-done | bytes 135200 | tf_op jit(solution)/shard_map/ppermute | solution.py:452
  177.8 2.7 %next_words.1.words_ref = bf16[2048,256]{1,0:T(8,128)(2,1)} custom-call(s32[1]{0:T(128)} %bitcast.30.where_ref, bf16[528,128]{1,0:T(8,128)(2,1)} %get-tuple-element.24.refs_0_, bf16[528,128]{1,0:T(8,128)(2,1)} %copy-done.12, bf16[528,128]{1,0:T(8,128)(2,1)} %copy-done.13, bf16[528,128]{1,0:T(8,128)(2,1)} %copy-done.14), custom_call_target="tpu_custom_call" | custom-call | tf_op jit(solution)/shard_map/next_words/pallas_call | solution.py:261
  180.5 32.2 %em_pass.3 = bf16[4,528,128]{2,1,0:T(8,128)(2,1)} custom-call(bf16[2048,256]{1,0:T(8,128)(2,1)} %next_words.1.words_ref, bf16[128,2048]{1,0:T(8,128)(2,1)} %copy-done.1, bf16[128,2048]{1,0:T(8,128)(2,1)} %get-tuple-element.22.refs_1_), custom_call_target="tpu_custom_call" | custom-call | tf_op jit(solution)/shard_map/em_pass/pallas_call | solution.py:361
  221.0 7.9 %collective-permute-done.22.refs_2_ = bf16[528,128]{1,0:T(8,128)(2,1)S(1)} collective-permute-done((bf16[528,128]{1,0:T(8,128)(2,1)S(1)}, bf16[528,128]{1,0:T(8,128)(2,1)S(1)}, u32[]{:S(2)}, u32[]{:S(2)}) %collective-permute-start.22) | collective-permute-done | bytes 135200 | tf_op jit(solution)/shard_map/ppermute | solution.py:452
  229.7 2.5 update.3
  240.0 7.2 %collective-permute-done.25.refs_2_ = bf16[512,128]{1,0:T(8,128)(2,1)S(1)} collective-permute-done((bf16[512,128]{1,0:T(8,128)(2,1)S(1)}, bf16[512,128]{1,0:T(8,128)(2,1)S(1)}, u32[]{:S(2)}, u32[]{:S(2)}) %collective-permute-start.25) | collective-permute-done | bytes 131104 | tf_op jit(solution)/shard_map/ppermute | solution.py:452
  254.3 3.4 %finish.1 = f32[2,2048,128]{2,1,0:T(8,128)} custom-call(s32[2]{0:T(128)} %pad_add_fusion.2.where_ref, bf16[512,128]{1,0:T(8,128)(2,1)} %copy-done.5, bf16[512,128]{1,0:T(8,128)(2,1)} %copy-done.28, bf16[512,128]{1,0:T(8,128)(2,1)} %copy-done.29, bf16[512,128]{1,0:T(8,128)(2,1)} %copy-done.30, bf16[512,128]{1,0:T(8,128)(2,1)} %copy-done.31, ...), custom_call_target="tpu_custom_call" | custom-call | tf_op jit(solution)/shard_map/finish/pallas_call | solution.py:428
  (128 shorter events, 50.1 us)
Async XLA Ops:
  5.1 13.9 %all-to-all-start.1 = ((s32[8,1,512]{2,1,0:T(1,128)}), s32[8,1,512]{2,1,0:T(1,128)S(1)}, u32[]{:S(2)}, u32[]{:S(2)}) async-start(s32[8,1,512]{2,1,0:T(1,128)} %copy.10), calls=%async_computation.1 | async-start | bytes 32768 | tf_op jit(solution)/shard_map/all_to_all | solution.py:460
  19.0 38.5 %all-to-all-start = ((bf16[512,4,256]{2,0,1:T(8,128)(2,1)}), bf16[512,4,256]{2,0,1:T(8,128)(2,1)S(1)}, u32[]{:S(2)}, u32[]{:S(2)}) async-start(bf16[512,4,256]{2,0,1:T(8,128)(2,1)} %bitcast.73), calls=%async_computation | async-start | bytes 2097152 | tf_op jit(solution)/shard_map/all_to_all | solution.py:459
  32.7 6.4 %collective-permute-start = (bf16[512,128]{1,0:T(8,128)(2,1)S(1)}, bf16[512,128]{1,0:T(8,128)(2,1)S(1)}, u32[]{:S(2)}, u32[]{:S(2)}) collective-permute-start(bf16[512,128]{1,0:T(8,128)(2,1)S(1)} %get-tuple-element.42), channel_id=1, source_target_pairs={{0,4},{4,0},{8,12},{12,8},{16,20},{20,16},{24,28},{28,24},{1,5},{5... | collective-permute-start | bytes 393224 | tf_op jit(solution)/shard_map/ppermute | solution.py:449
  33.2 8.0 %collective-permute-start.1 = (bf16[512,128]{1,0:T(8,128)(2,1)S(1)}, bf16[512,128]{1,0:T(8,128)(2,1)S(1)}, u32[]{:S(2)}, u32[]{:S(2)}) collective-permute-start(bf16[512,128]{1,0:T(8,128)(2,1)S(1)} %get-tuple-element.41), channel_id=1, source_target_pairs={{0,8},{4,12},{8,0},{12,4},{16,24},{20,28},{24,16},{28,20},{1,9},{5... | collective-permute-start | bytes 393224 | tf_op jit(solution)/shard_map/ppermute | solution.py:449
  33.8 12.4 %collective-permute-start.2 = (bf16[512,128]{1,0:T(8,128)(2,1)S(1)}, bf16[512,128]{1,0:T(8,128)(2,1)S(1)}, u32[]{:S(2)}, u32[]{:S(2)}) collective-permute-start(bf16[512,128]{1,0:T(8,128)(2,1)S(1)} %get-tuple-element.40), channel_id=1, source_target_pairs={{0,12},{4,8},{8,4},{12,0},{16,28},{20,24},{24,20},{28,16},{1,13},{... | collective-permute-start | bytes 393224 | tf_op jit(solution)/shard_map/ppermute | solution.py:449
  36.2 18.5 %collective-permute-start.3 = (bf16[512,128]{1,0:T(8,128)(2,1)S(1)}, bf16[512,128]{1,0:T(8,128)(2,1)S(1)}, u32[]{:S(2)}, u32[]{:S(2)}) collective-permute-start(bf16[512,128]{1,0:T(8,128)(2,1)S(1)} %get-tuple-element.39), channel_id=1, source_target_pairs={{0,16},{4,20},{8,24},{12,28},{16,0},{20,4},{24,8},{28,12},{1,17},{... | collective-permute-start | bytes 393224 | tf_op jit(solution)/shard_map/ppermute | solution.py:449
  36.7 20.7 %collective-permute-start.4 = (bf16[512,128]{1,0:T(8,128)(2,1)S(1)}, bf16[512,128]{1,0:T(8,128)(2,1)S(1)}, u32[]{:S(2)}, u32[]{:S(2)}) collective-permute-start(bf16[512,128]{1,0:T(8,128)(2,1)S(1)} %get-tuple-element.38), channel_id=1, source_target_pairs={{0,20},{4,16},{8,28},{12,24},{16,4},{20,0},{24,12},{28,8},{1,21},{... | collective-permute-start | bytes 393224 | tf_op jit(solution)/shard_map/ppermute | solution.py:449
  39.1 18.4 %collective-permute-start.5 = (bf16[512,128]{1,0:T(8,128)(2,1)S(1)}, bf16[512,128]{1,0:T(8,128)(2,1)S(1)}, u32[]{:S(2)}, u32[]{:S(2)}) collective-permute-start(bf16[512,128]{1,0:T(8,128)(2,1)S(1)} %get-tuple-element.37), channel_id=1, source_target_pairs={{0,24},{4,28},{8,16},{12,20},{16,8},{20,12},{24,0},{28,4},{1,25},{... | collective-permute-start | bytes 393224 | tf_op jit(solution)/shard_map/ppermute | solution.py:449
  41.3 16.2 %collective-permute-start.6 = (bf16[512,128]{1,0:T(8,128)(2,1)S(1)}, bf16[512,128]{1,0:T(8,128)(2,1)}, u32[]{:S(2)}, u32[]{:S(2)}) collective-permute-start(bf16[512,128]{1,0:T(8,128)(2,1)S(1)} %get-tuple-element.36), channel_id=1, source_target_pairs={{0,28},{4,24},{8,20},{12,16},{16,12},{20,8},{24,4},{28,0},{1,29},{... | collective-permute-start | bytes 393224 | tf_op jit(solution)/shard_map/ppermute | solution.py:449
  65.0 43.8 %collective-permute-start.14 = (bf16[128,2048]{1,0:T(8,128)(2,1)}, bf16[128,2048]{1,0:T(8,128)(2,1)S(1)}, u32[]{:S(2)}, u32[]{:S(2)}) collective-permute-start(bf16[128,2048]{1,0:T(8,128)(2,1)} %get-tuple-element.21), channel_id=1, source_target_pairs={{0,4},{4,0},{8,12},{12,8},{16,20},{20,16},{24,28},{28,24},{1,5},{5... | collective-permute-start | bytes 1572872 | tf_op jit(solution)/shard_map/ppermute | solution.py:456
  67.2 14.8 %collective-permute-start.7 = (bf16[512,128]{1,0:T(8,128)(2,1)S(1)}, bf16[512,128]{1,0:T(8,128)(2,1)S(1)}, u32[]{:S(2)}, u32[]{:S(2)}) collective-permute-start(bf16[512,128]{1,0:T(8,128)(2,1)S(1)} %get-tuple-element.34), channel_id=1, source_target_pairs={{0,4},{4,0},{8,12},{12,8},{16,20},{20,16},{24,28},{28,24},{1,5},{5... | collective-permute-start | bytes 393224 | tf_op jit(solution)/shard_map/ppermute | solution.py:449
  67.8 21.1 %collective-permute-start.8 = (bf16[512,128]{1,0:T(8,128)(2,1)S(1)}, bf16[512,128]{1,0:T(8,128)(2,1)S(1)}, u32[]{:S(2)}, u32[]{:S(2)}) collective-permute-start(bf16[512,128]{1,0:T(8,128)(2,1)S(1)} %get-tuple-element.33), channel_id=1, source_target_pairs={{0,8},{4,12},{8,0},{12,4},{16,24},{20,28},{24,16},{28,20},{1,9},{5... | collective-permute-start | bytes 393224 | tf_op jit(solution)/shard_map/ppermute | solution.py:449
  72.6 19.0 %collective-permute-start.9 = (bf16[512,128]{1,0:T(8,128)(2,1)S(1)}, bf16[512,128]{1,0:T(8,128)(2,1)S(1)}, u32[]{:S(2)}, u32[]{:S(2)}) collective-permute-start(bf16[512,128]{1,0:T(8,128)(2,1)S(1)} %get-tuple-element.32), channel_id=1, source_target_pairs={{0,12},{4,8},{8,4},{12,0},{16,28},{20,24},{24,20},{28,16},{1,13},{... | collective-permute-start | bytes 393224 | tf_op jit(solution)/shard_map/ppermute | solution.py:449
  73.6 21.6 %collective-permute-start.10 = (bf16[512,128]{1,0:T(8,128)(2,1)S(1)}, bf16[512,128]{1,0:T(8,128)(2,1)S(1)}, u32[]{:S(2)}, u32[]{:S(2)}) collective-permute-start(bf16[512,128]{1,0:T(8,128)(2,1)S(1)} %get-tuple-element.31), channel_id=1, source_target_pairs={{0,16},{4,20},{8,24},{12,28},{16,0},{20,4},{24,8},{28,12},{1,17},{... | collective-permute-start | bytes 393224 | tf_op jit(solution)/shard_map/ppermute | solution.py:449
  82.1 19.3 %collective-permute-start.11 = (bf16[512,128]{1,0:T(8,128)(2,1)S(1)}, bf16[512,128]{1,0:T(8,128)(2,1)S(1)}, u32[]{:S(2)}, u32[]{:S(2)}) collective-permute-start(bf16[512,128]{1,0:T(8,128)(2,1)S(1)} %get-tuple-element.30), channel_id=1, source_target_pairs={{0,20},{4,16},{8,28},{12,24},{16,4},{20,0},{24,12},{28,8},{1,21},{... | collective-permute-start | bytes 393224 | tf_op jit(solution)/shard_map/ppermute | solution.py:449
  88.9 12.5 %collective-permute-start.12 = (bf16[512,128]{1,0:T(8,128)(2,1)S(1)}, bf16[512,128]{1,0:T(8,128)(2,1)S(1)}, u32[]{:S(2)}, u32[]{:S(2)}) collective-permute-start(bf16[512,128]{1,0:T(8,128)(2,1)S(1)} %get-tuple-element.29), channel_id=1, source_target_pairs={{0,24},{4,28},{8,16},{12,20},{16,8},{20,12},{24,0},{28,4},{1,25},{... | collective-permute-start | bytes 393224 | tf_op jit(solution)/shard_map/ppermute | solution.py:449
  91.6 9.8 %collective-permute-start.13 = (bf16[512,128]{1,0:T(8,128)(2,1)S(1)}, bf16[512,128]{1,0:T(8,128)(2,1)S(1)}, u32[]{:S(2)}, u32[]{:S(2)}) collective-permute-start(bf16[512,128]{1,0:T(8,128)(2,1)S(1)} %get-tuple-element.28), channel_id=1, source_target_pairs={{0,28},{4,24},{8,20},{12,16},{16,12},{20,8},{24,4},{28,0},{1,29},{... | collective-permute-start | bytes 393224 | tf_op jit(solution)/shard_map/ppermute | solution.py:449
  143.4 8.2 %collective-permute-start.15 = (bf16[528,128]{1,0:T(8,128)(2,1)S(1)}, bf16[528,128]{1,0:T(8,128)(2,1)S(1)}, u32[]{:S(2)}, u32[]{:S(2)}) collective-permute-start(bf16[528,128]{1,0:T(8,128)(2,1)S(1)} %get-tuple-element.50), channel_id=1, source_target_pairs={{0,8},{4,12},{8,0},{12,4},{16,24},{20,28},{24,16},{28,20},{1,9},{5... | collective-permute-start | bytes 405512 | tf_op jit(solution)/shard_map/ppermute | solution.py:452
  147.6 11.6 %collective-permute-start.16 = (bf16[528,128]{1,0:T(8,128)(2,1)S(1)}, bf16[528,128]{1,0:T(8,128)(2,1)S(1)}, u32[]{:S(2)}, u32[]{:S(2)}) collective-permute-start(bf16[528,128]{1,0:T(8,128)(2,1)S(1)} %get-tuple-element.49), channel_id=1, source_target_pairs={{0,16},{4,20},{8,24},{12,28},{16,0},{20,4},{24,8},{28,12},{1,17},{... | collective-permute-start | bytes 405512 | tf_op jit(solution)/shard_map/ppermute | solution.py:452
  148.2 10.9 %collective-permute-start.17 = (bf16[528,128]{1,0:T(8,128)(2,1)S(1)}, bf16[528,128]{1,0:T(8,128)(2,1)S(1)}, u32[]{:S(2)}, u32[]{:S(2)}) collective-permute-start(bf16[528,128]{1,0:T(8,128)(2,1)S(1)} %get-tuple-element.48), channel_id=1, source_target_pairs={{0,24},{4,28},{8,16},{12,20},{16,8},{20,12},{24,0},{28,4},{1,25},{... | collective-permute-start | bytes 405512 | tf_op jit(solution)/shard_map/ppermute | solution.py:452
  162.3 6.7 %collective-permute-start.18 = (bf16[528,128]{1,0:T(8,128)(2,1)}, bf16[528,128]{1,0:T(8,128)(2,1)S(1)}, u32[]{:S(2)}, u32[]{:S(2)}) collective-permute-start(bf16[528,128]{1,0:T(8,128)(2,1)} %get-tuple-element.24.refs_0_), channel_id=1, source_target_pairs={{0,8},{4,12},{8,0},{12,4},{16,24},{20,28},{24,16},{28,20},{1,9},{5... | collective-permute-start | bytes 405512 | tf_op jit(solution)/shard_map/ppermute | solution.py:452
  164.3 12.8 %collective-permute-start.19 = (bf16[528,128]{1,0:T(8,128)(2,1)}, bf16[528,128]{1,0:T(8,128)(2,1)S(1)}, u32[]{:S(2)}, u32[]{:S(2)}) collective-permute-start(bf16[528,128]{1,0:T(8,128)(2,1)} %get-tuple-element.24.refs_0_), channel_id=1, source_target_pairs={{0,16},{4,20},{8,24},{12,28},{16,0},{20,4},{24,8},{28,12},{1,17},{... | collective-permute-start | bytes 405512 | tf_op jit(solution)/shard_map/ppermute | solution.py:452
  165.2 11.9 %collective-permute-start.20 = (bf16[528,128]{1,0:T(8,128)(2,1)}, bf16[528,128]{1,0:T(8,128)(2,1)S(1)}, u32[]{:S(2)}, u32[]{:S(2)}) collective-permute-start(bf16[528,128]{1,0:T(8,128)(2,1)} %get-tuple-element.24.refs_0_), channel_id=1, source_target_pairs={{0,24},{4,28},{8,16},{12,20},{16,8},{20,12},{24,0},{28,4},{1,25},{... | collective-permute-start | bytes 405512 | tf_op jit(solution)/shard_map/ppermute | solution.py:452
  214.5 6.5 %collective-permute-start.21 = (bf16[528,128]{1,0:T(8,128)(2,1)S(1)}, bf16[528,128]{1,0:T(8,128)(2,1)S(1)}, u32[]{:S(2)}, u32[]{:S(2)}) collective-permute-start(bf16[528,128]{1,0:T(8,128)(2,1)S(1)} %get-tuple-element.46), channel_id=1, source_target_pairs={{0,8},{4,12},{8,0},{12,4},{16,24},{20,28},{24,16},{28,20},{1,9},{5... | collective-permute-start | bytes 405512 | tf_op jit(solution)/shard_map/ppermute | solution.py:452
  216.5 12.5 %collective-permute-start.22 = (bf16[528,128]{1,0:T(8,128)(2,1)S(1)}, bf16[528,128]{1,0:T(8,128)(2,1)S(1)}, u32[]{:S(2)}, u32[]{:S(2)}) collective-permute-start(bf16[528,128]{1,0:T(8,128)(2,1)S(1)} %get-tuple-element.45), channel_id=1, source_target_pairs={{0,16},{4,20},{8,24},{12,28},{16,0},{20,4},{24,8},{28,12},{1,17},{... | collective-permute-start | bytes 405512 | tf_op jit(solution)/shard_map/ppermute | solution.py:452
  217.4 11.6 %collective-permute-start.23 = (bf16[528,128]{1,0:T(8,128)(2,1)S(1)}, bf16[528,128]{1,0:T(8,128)(2,1)S(1)}, u32[]{:S(2)}, u32[]{:S(2)}) collective-permute-start(bf16[528,128]{1,0:T(8,128)(2,1)S(1)} %get-tuple-element.44), channel_id=1, source_target_pairs={{0,24},{4,28},{8,16},{12,20},{16,8},{20,12},{24,0},{28,4},{1,25},{... | collective-permute-start | bytes 405512 | tf_op jit(solution)/shard_map/ppermute | solution.py:452
  233.0 6.4 %collective-permute-start.24 = (bf16[512,128]{1,0:T(8,128)(2,1)S(1)}, bf16[512,128]{1,0:T(8,128)(2,1)S(1)}, u32[]{:S(2)}, u32[]{:S(2)}) collective-permute-start(bf16[512,128]{1,0:T(8,128)(2,1)S(1)} %slice.3.refs_0_), channel_id=1, source_target_pairs={{0,8},{4,12},{8,0},{12,4},{16,24},{20,28},{24,16},{28,20},{1,9},{5... | collective-permute-start | bytes 393224 | tf_op jit(solution)/shard_map/ppermute | solution.py:452
  235.1 12.1 %collective-permute-start.25 = (bf16[512,128]{1,0:T(8,128)(2,1)S(1)}, bf16[512,128]{1,0:T(8,128)(2,1)S(1)}, u32[]{:S(2)}, u32[]{:S(2)}) collective-permute-start(bf16[512,128]{1,0:T(8,128)(2,1)S(1)} %slice.3.refs_0_), channel_id=1, source_target_pairs={{0,16},{4,20},{8,24},{12,28},{16,0},{20,4},{24,8},{28,12},{1,17},{... | collective-permute-start | bytes 393224 | tf_op jit(solution)/shard_map/ppermute | solution.py:452
  236.0 11.2 %collective-permute-start.26 = (bf16[512,128]{1,0:T(8,128)(2,1)S(1)}, bf16[512,128]{1,0:T(8,128)(2,1)S(1)}, u32[]{:S(2)}, u32[]{:S(2)}) collective-permute-start(bf16[512,128]{1,0:T(8,128)(2,1)S(1)} %slice.3.refs_0_), channel_id=1, source_target_pairs={{0,24},{4,28},{8,16},{12,20},{16,8},{20,12},{24,0},{28,4},{1,25},{... | collective-permute-start | bytes 393224 | tf_op jit(solution)/shard_map/ppermute | solution.py:452
  237.9 12.4 %collective-permute-start.27 = (bf16[512,128]{1,0:T(8,128)(2,1)S(1)}, bf16[512,128]{1,0:T(8,128)(2,1)S(1)}, u32[]{:S(2)}, u32[]{:S(2)}) collective-permute-start(bf16[512,128]{1,0:T(8,128)(2,1)S(1)} %slice.3.refs_0_), channel_id=1, source_target_pairs={{0,4},{4,0},{8,12},{12,8},{16,20},{20,16},{24,28},{28,24},{1,5},{5... | collective-permute-start | bytes 393224 | tf_op jit(solution)/shard_map/ppermute | solution.py:456
  239.5 10.9 %collective-permute-start.28 = (bf16[512,128]{1,0:T(8,128)(2,1)S(1)}, bf16[512,128]{1,0:T(8,128)(2,1)S(1)}, u32[]{:S(2)}, u32[]{:S(2)}) collective-permute-start(bf16[512,128]{1,0:T(8,128)(2,1)S(1)} %collective-permute-done.24.refs_1_), channel_id=1, source_target_pairs={{0,4},{4,0},{8,12},{12,8},{16,20},{20,16},{24,28},{28,24},{1,5},{5... | collective-permute-start | bytes 393224 | tf_op jit(solution)/shard_map/ppermute | solution.py:456
  247.2 6.4 %collective-permute-start.30 = (bf16[512,128]{1,0:T(8,128)(2,1)S(1)}, bf16[512,128]{1,0:T(8,128)(2,1)S(1)}, u32[]{:S(2)}, u32[]{:S(2)}) collective-permute-start(bf16[512,128]{1,0:T(8,128)(2,1)S(1)} %collective-permute-done.26.refs_3_), channel_id=1, source_target_pairs={{0,4},{4,0},{8,12},{12,8},{16,20},{20,16},{24,28},{28,24},{1,5},{5... | collective-permute-start | bytes 393224 | tf_op jit(solution)/shard_map/ppermute | solution.py:456
  (36 other events, 337.2 us)
